TPU v7x, 32 devices: a whole 2x2x4 slice. The times are simulated.
32 devices in a mesh: harm: 8 (over y, x, core), mode: 4 (over z).
Axes of the slice: x: 2, y: 2, z: 4, core: 2. Of those that a mesh axis runs over, the one named last changes fastest.
Arguments:
- mode_vectors: float32 [49152, 1024], P('harm', 'mode'), may hold values from -0.09375 to 0.09375
- weights: float32 [49152, 1024], P('harm', 'mode'), may hold values from -0.1875 to 0.1875
- cotangent: float32 [49152, 1024], P('harm', 'mode'), may hold values from -6 to 6
- eigenvalues: float32 [1024], replicated, may hold values from 0 to 4
- eigen_cotangent: float32 [1024], replicated, may hold values from -6 to 6
- slab_rows: int32 [4096], replicated, may hold values from 0 to 49151, as said below
Outputs:
- slab: float32 [4096, 49152], P('mode', 'harm')
Inputs may be any that keep to these rules, and one draw needn't show every extreme that they name: `slab_rows`: each block of 6144 consecutive harmonics (0 to 6143, 6144 to 12287 and so on) holds exactly 512 of the slab rows.
All inputs are finite; a program needn't handle non-finite values.
Results may differ from a plain program's by a relative error of at most 0.0001.
Values sent between devices are 32-bit elements; how exact they have to be, the bound alone decides.
A program may use at most 128 MiB of HBM per device.

v0:
```python
import jax
import jax.numpy as jnp
from jax import lax
from jax.sharding import PartitionSpec as P

regular = 0.01
precision = lax.Precision.HIGHEST


def product(left, right, left_dim, right_dim):
    return lax.dot_general(
        left,
        right,
        (((left_dim,), (right_dim,)), ((), ())),
        precision=precision,
        preferred_element_type=jnp.float32,
    )


def weigh_gap(block, row_ids, col_ids, eigenvalues, eigen_cotangent):
    eigen_rows = lax.dynamic_slice_in_dim(eigenvalues, row_ids, block.shape[0])
    eigen_cols = lax.dynamic_slice_in_dim(eigenvalues, col_ids, block.shape[1])
    slope_cols = lax.dynamic_slice_in_dim(eigen_cotangent, col_ids, block.shape[1])
    differ = eigen_cols[None, :] - eigen_rows[:, None]
    factor = differ / (differ * differ + regular)
    rows = row_ids + lax.broadcasted_iota(jnp.int32, block.shape, 0)
    cols = col_ids + lax.broadcasted_iota(jnp.int32, block.shape, 1)
    return factor * block + jnp.where(rows == cols, slope_cols[None, :], 0.0)


def pick_rows(table, slab_rows, harm_index):
    row_count = table.shape[0]
    offset = slab_rows - harm_index * row_count
    inside = (offset >= 0) & (offset < row_count)
    picked = jnp.take(table, jnp.clip(offset, 0, row_count - 1), axis=0)
    return jnp.where(inside[:, None], picked, 0.0)


def gather_weights(weights, slab_rows, harm_index, harm_count, mode_count):
    width = weights.shape[1]
    with jax.named_scope("pick"):
        picked = pick_rows(weights, slab_rows, harm_index)
    piece = slab_rows.shape[0] // (harm_count * mode_count)
    picked = picked.reshape(mode_count, harm_count, piece, width)
    with jax.named_scope("sum_weights"):
        picked = lax.psum_scatter(picked, "harm", scatter_dimension=1, tiled=True)
    picked = picked.reshape(mode_count, piece, width)
    with jax.named_scope("swap"):
        swapped = lax.all_to_all(picked, "mode", split_axis=0, concat_axis=2, tiled=True)
    with jax.named_scope("spread_weights"):
        return lax.all_gather(
            swapped.reshape(piece, mode_count * width), "harm", axis=0, tiled=True
        )


def plain(
    mode_vectors,
    weights,
    cotangent,
    eigenvalues,
    eigen_cotangent,
    slab_rows,
    harm_count,
    mode_count,
):
    harm_index = lax.axis_index("harm")
    width = mode_vectors.shape[1]
    modes = width * mode_count
    full = lax.all_gather(mode_vectors, "mode", axis=1, tiled=True)
    owned_weights = gather_weights(weights, slab_rows, harm_index, harm_count, mode_count)
    gram = product(full, cotangent, 0, 0)
    gram = lax.psum_scatter(gram, "harm", scatter_dimension=0, tiled=True)
    weighted = weigh_gap(
        gram,
        harm_index * (modes // harm_count),
        lax.axis_index("mode") * width,
        eigenvalues,
        eigen_cotangent,
    )
    weighted = lax.all_gather(weighted, "mode", axis=1, tiled=True)
    weighted = lax.all_gather(weighted, "harm", axis=0, tiled=True)
    return product(product(owned_weights, weighted, 1, 0), full, 1, 1)


def solution(mesh):
    harm_count = mesh.shape["harm"]
    mode_count = mesh.shape["mode"]
    placed = (P("harm", "mode"), P("harm", "mode"), P("harm", "mode"), P(), P(), P())

    def local(*operands):
        return plain(*operands, harm_count, mode_count)

    return jax.shard_map(
        local, mesh=mesh, in_specs=placed, out_specs=P("mode", "harm"), check_vma=False
    )
```

profile of v0, /device:TPU:0, one launch (start us, length us, event | category | flops | bytes accessed | tf_op | source)
XLA Modules:
  0.0 702.6 jit_solution(5876162007898497041)
XLA Ops:
  7.4 0.0 copy-start
  7.4 0.0 all-gather.6.cloned.1.call-start
  7.4 0.7 all-gather.6.cloned.1.call-update
  8.1 0.0 reduce-scatter.3.cloned.1.call-start
  8.1 0.0 copy-done
  8.2 18.9 %gather_fusion = f32[4096,256]{1,0:T(8,128)} fusion(f32[6144,256]{1,0:T(8,128)} %param.7, s32[4096]{0:T(1024)S(1)} %fusion.3), kind=kCustom, calls=%fused_computation | custom fusion | bytes 8404992 | tf_op jit(solution)/shard_map/pick/jit(_take)/gather | solution.py:35
  27.2 5.6 copy.10
  32.7 5.5 select_select_fusion
  38.3 0.0 reduce-scatter.3.cloned.1.call-update
  38.3 0.0 reduce-scatter.5.cloned.1.call-start
  38.3 399.3 %all-gather.6.cloned.1.call-done = f32[6144,1024]{1,0:T(8,128)} async-done(((f32[6144,256]{1,0:T(8,128)}), f32[6144,1024]{1,0:T(8,128)}) %all-gather.6.cloned.1.call-update) | async-done | bytes 25165840 | tf_op jit(solution)/shard_map/all_gather | solution.py:69
  437.7 44.0 %fusion.4 = f32[1024,256]{1,0:T(8,128)} fusion(f32[6144,1024]{1,0:T(8,128)} %all-gather.6.cloned.1.call-done, f32[6144,256]{1,0:T(8,128)} %param.8), kind=kOutput, calls=%fused_computation.13 | convolution fusion | flops 19327352832 | bytes 32505856 | tf_op jit(solution)/shard_map/dot_general | solution.py:11
  481.6 0.0 reduce-scatter.5.cloned.1.call-update
  481.6 0.0 all-gather.4.cloned.1.call-start
  481.7 0.0 reduce-scatter.3.cloned.1.call-done
  481.7 19.2 %all_to_all.15 = f32[4,128,256]{1,2,0:T(8,128)} all-to-all(f32[4,128,256]{1,2,0:T(8,128)} %bitcast.19), channel_id=1, replica_groups=mesh['harm'=8,'mode'=4] {'mode'}, dimensions={0} | all-to-all | bytes 1048576 | tf_op jit(solution)/shard_map/swap/all_to_all | solution.py:49
  500.9 0.0 all-gather.4.cloned.1.call-update
  500.9 0.0 all-gather.8.cloned.1.call-start
  501.0 0.8 dynamic_slice.10
  501.7 0.8 dynamic_slice.9
  502.5 0.8 dynamic_slice.11
  503.2 12.6 %reduce-scatter.5.cloned.1.call-done = f32[128,256]{1,0:T(8,128)} async-done(((f32[1024,256]{1,0:T(8,128)}), f32[128,256]{1,0:T(8,128)}) %reduce-scatter.5.cloned.1.call-update) | async-done | bytes 131088 | tf_op jit(solution)/shard_map/reduce_scatter | solution.py:72
  515.8 1.0 fusion.2
  516.9 15.9 %all_gather.14 = f32[128,1024]{1,0:T(8,128)} all-gather(f32[128,256]{1,0:T(8,128)S(1)} %fusion.2), channel_id=1, replica_groups=mesh['harm'=8,'mode'=4] {'mode'}, dimensions={1}, use_global_device_ids=true | all-gather | bytes 655360 | tf_op jit(solution)/shard_map/all_gather | solution.py:80
  532.8 0.0 all-gather.8.cloned.1.call-update
  532.8 22.0 %all-gather.4.cloned.1.call-done = f32[1024,1024]{0,1:T(8,128)} async-done(((f32[128,1024]{0,1:T(8,128)}), f32[1024,1024]{0,1:T(8,128)}) %all-gather.4.cloned.1.call-update) | async-done | bytes 4194320 | tf_op jit(solution)/shard_map/spread_weights/all_gather | solution.py:51
  554.8 38.4 %all-gather.8.cloned.1.call-done = f32[1024,1024]{1,0:T(8,128)} async-done(((f32[128,1024]{1,0:T(8,128)}), f32[1024,1024]{1,0:T(8,128)}) %all-gather.8.cloned.1.call-update) | async-done | bytes 4194320 | tf_op jit(solution)/shard_map/all_gather | solution.py:81
  593.2 16.6 %fusion.5 = f32[1024,1024]{1,0:T(8,128)S(1)} fusion(f32[1024,1024]{0,1:T(8,128)} %all-gather.4.cloned.1.call-done, f32[1024,1024]{1,0:T(8,128)} %all-gather.8.cloned.1.call-done), kind=kOutput, calls=%fused_computation.14 | convolution fusion | flops 12884901888 | bytes 12582912 | tf_op jit(solution)/shard_map/dot_general | solution.py:11
  609.8 85.2 %fusion.6 = f32[1024,6144]{1,0:T(8,128)} fusion(f32[1024,1024]{1,0:T(8,128)S(1)} %fusion.5, f32[6144,1024]{1,0:T(8,128)} %all-gather.6.cloned.1.call-done), kind=kOutput, calls=%fused_computation.15 | convolution fusion | flops 77309411328 | bytes 54525952 | tf_op jit(solution)/shard_map/dot_general | solution.py:11
  (6 shorter events, 0.1 us)
Async XLA Ops:
  7.4 0.8 copy-start
  7.4 430.3 %all-gather.6.cloned.1.call-start = ((), (), s32[]{:S(2)}) async-start(), calls=%async_computation.5 | async-start | bytes 31457280 | tf_op jit(solution)/shard_map/all_gather | solution.py:69
  8.1 473.6 %reduce-scatter.3.cloned.1.call-start = ((), (), s32[]{:S(2)}) async-start(), calls=%async_computation.3 | async-start | bytes 4718592 | tf_op jit(solution)/shard_map/sum_weights/reduce_scatter | solution.py:46
  38.3 477.6 %reduce-scatter.5.cloned.1.call-start = ((), (), s32[]{:S(2)}) async-start(), calls=%async_computation.6 | async-start | bytes 1179648 | tf_op jit(solution)/shard_map/reduce_scatter | solution.py:72
  481.6 73.2 %all-gather.4.cloned.1.call-start = ((), (), s32[]{:S(2)}) async-start(), calls=%async_computation.4 | async-start | bytes 4718592 | tf_op jit(solution)/shard_map/spread_weights/all_gather | solution.py:51
  500.9 92.3 %all-gather.8.cloned.1.call-start = ((), (), s32[]{:S(2)}) async-start(), calls=%async_computation.7 | async-start | bytes 4718592 | tf_op jit(solution)/shard_map/all_gather | solution.py:81
Sparse Core Ops, SparseCore 0:
  9.7 427.8 all-gather.5
Sparse Core Ops, SparseCore 1:
  38.4 53.7 reduce-scatter.2
  481.7 34.1 reduce-scatter.4
  517.6 37.2 all-gather.3
  556.8 36.4 all-gather.7
where the time goes:
time: 703 us
  waiting for transfers between devices  473 us (67%)
  matrix products  146 us (21%)
  blocking collectives  35.1 us (5%)
  local copies, waits for them, and re-layouts  26.8 us (4%)
  between operations  15.1 us (2%)
    all_gather x1, waiting for transfers between devices, plain(): full = lax.all_gather(mode_vectors, 'mode', axis=1, tiled=True)  399 us
    dot_general x3, matrix products, product(): lax.dot_general(left, right, (((left_dim,), (right_dim,)), ((), ())), pre...  146 us
    all_gather x1, waiting for transfers between devices, plain(): weighted = lax.all_gather(weighted, 'harm', axis=0, tiled=True)  38.4 us
    gather x2, local copies, waits for them, and re-layouts, pick_rows(): picked = jnp.take(table, jnp.clip(offset, 0, row_count - 1), axis=0)  24.5 us
    all_gather x1, waiting for transfers between devices, gather_weights(): lax.all_gather(swapped.reshape(piece, mode_count * width), 'harm', axis=0...  22 us
    all_to_all x1, blocking collectives, gather_weights(): lax.all_to_all(picked, 'mode', split_axis=0, concat_axis=2, tiled=True)  19.2 us
    all_gather x1, blocking collectives, plain(): weighted = lax.all_gather(weighted, 'mode', axis=1, tiled=True)  15.9 us
  transfers between devices with their start and end apart: 5, of which 4 were waited for; matrix products, arithmetic and copies ran while one was open for 11% of the time, Pallas kernels for 0%

commit v1 on v0

--- a/solution.py
+++ b/solution.py
@@ -5,6 +5,28 @@
 
 regular = 0.01
 precision = lax.Precision.HIGHEST
+
+
+def in_blocks(value, dim, devices):
+    before, after = (value.shape[:dim], value.shape[dim + 1 :])
+    return jnp.moveaxis(value.reshape(*before, devices, -1, *after), dim, 0)
+
+
+def in_order(blocks, dim):
+    dims = list(blocks.shape[1:])
+    dims[dim] *= blocks.shape[0]
+    return jnp.moveaxis(blocks, 0, dim).reshape(dims)
+
+
+def pairwise_exchange(array, axis, split_dim, concat_dim):
+    size, index = (lax.axis_size(axis), lax.axis_index(axis))
+    parts = in_blocks(array, split_dim, size)
+    outs = [parts[index]]
+    for step in range(1, size):
+        sent = parts[index ^ step]
+        outs.append(lax.ppermute(sent, axis, [(i, i ^ step) for i in range(size)]))
+    parts = jnp.stack(outs)[index ^ jnp.arange(size)]
+    return in_order(parts, concat_dim)
 
 
 def product(left, right, left_dim, right_dim):
@@ -46,7 +68,7 @@
         picked = lax.psum_scatter(picked, "harm", scatter_dimension=1, tiled=True)
     picked = picked.reshape(mode_count, piece, width)
     with jax.named_scope("swap"):
-        swapped = lax.all_to_all(picked, "mode", split_axis=0, concat_axis=2, tiled=True)
+        swapped = pairwise_exchange(picked, "mode", 0, 2)
     with jax.named_scope("spread_weights"):
         return lax.all_gather(
             swapped.reshape(piece, mode_count * width), "harm", axis=0, tiled=True

time: 703 us -> 703 us (level)
  blocking collectives: 35.1 us -> 16.1 us
  waiting for transfers between devices: 473 us -> 490 us
    all_to_all x1 -> x0, blocking collectives: 19.2 us -> none  [gather_weights(): lax.all_to_all(picked, 'mode', split_axis=0, concat_axis=2, tiled=True)]
    ppermute x0 -> x3, waiting for transfers between devices: none -> 7.98 us  [pairwise_exchange(): outs.append(lax.ppermute(sent, axis, [(i, i ^ step) for i in range(size)]))]
    gather x2 -> x1, local copies, waits for them, and re-layouts: 24.5 us -> 18.9 us  [pick_rows(): picked = jnp.take(table, jnp.clip(offset, 0, row_count - 1), axis=0)]
  transfers between devices with their start and end apart: 5 -> 8, of which waited for: 4 -> 6; matrix products, arithmetic and copies ran while one was open for 11% -> 11% of each run, Pallas kernels for 0% -> 0%
where the time goes in v1:
time: 703 us
  waiting for transfers between devices  490 us (70%)
  matrix products  146 us (21%)
  local copies, waits for them, and re-layouts  23.9 us (3%)
  blocking collectives  16.1 us (2%)
  between operations  15.2 us (2%)
    all_gather x1, waiting for transfers between devices, plain(): full = lax.all_gather(mode_vectors, 'mode', axis=1, tiled=True)  405 us
    dot_general x3, matrix products, product(): lax.dot_general(left, right, (((left_dim,), (right_dim,)), ((), ())), pre...  146 us
    all_gather x1, waiting for transfers between devices, plain(): weighted = lax.all_gather(weighted, 'harm', axis=0, tiled=True)  38.4 us
    all_gather x1, waiting for transfers between devices, gather_weights(): lax.all_gather(swapped.reshape(piece, mode_count * width), 'harm', axis=0...  21.8 us
    gather x1, local copies, waits for them, and re-layouts, pick_rows(): picked = jnp.take(table, jnp.clip(offset, 0, row_count - 1), axis=0)  18.9 us
    reduce_scatter x1, waiting for transfers between devices, plain(): gram = lax.psum_scatter(gram, 'harm', scatter_dimension=0, tiled=True)  16.5 us
    all_gather x1, blocking collectives, plain(): weighted = lax.all_gather(weighted, 'mode', axis=1, tiled=True)  16.1 us
  transfers between devices with their start and end apart: 8, of which 6 were waited for; matrix products, arithmetic and copies ran while one was open for 11% of the time, Pallas kernels for 0%

profile of v1, /device:TPU:0, one launch (start us, length us, event | category | flops | bytes accessed | tf_op | source)
XLA Modules:
  0.0 702.6 jit_solution(2700233737331766487)
XLA Ops:
  7.4 0.7 all-gather.6.cloned.1.call-update
  8.1 0.0 reduce-scatter.3.cloned.1.call-start
  8.2 18.9 %gather_fusion = f32[4096,256]{1,0:T(8,128)} fusion(f32[6144,256]{1,0:T(8,128)} %param.7, s32[4096]{0:T(1024)S(1)} %fusion.4), kind=kCustom, calls=%fused_computation | custom fusion | bytes 8404992 | tf_op jit(solution)/shard_map/pick/jit(_take)/gather | solution.py:57
  27.2 5.5 fusion
  32.7 0.0 reduce-scatter.3.cloned.1.call-update
  32.7 0.0 reduce-scatter.5.cloned.1.call-start
  32.7 404.9 %all-gather.6.cloned.1.call-done = f32[6144,1024]{1,0:T(8,128)} async-done(((f32[6144,256]{1,0:T(8,128)}), f32[6144,1024]{1,0:T(8,128)}) %all-gather.6.cloned.1.call-update) | async-done | bytes 25165840 | tf_op jit(solution)/shard_map/all_gather | solution.py:91
  437.7 43.9 %fusion.6 = f32[1024,256]{1,0:T(8,128)} fusion(f32[6144,1024]{1,0:T(8,128)} %all-gather.6.cloned.1.call-done, f32[6144,256]{1,0:T(8,128)} %param.8), kind=kOutput, calls=%fused_computation.23 | convolution fusion | flops 19327352832 | bytes 32505856 | tf_op jit(solution)/shard_map/dot_general | solution.py:33
  481.5 0.0 reduce-scatter.5.cloned.1.call-update
  481.6 0.0 all-gather.4.cloned.1.call-start
  481.6 0.0 reduce-scatter.3.cloned.1.call-done
  481.7 1.1 constant_dynamic-slice_fusion
  482.8 0.4 collective-permute-start.2
  483.2 0.4 collective-permute-start.1
  483.6 3.7 collective-permute-start
  487.3 3.9 collective-permute-done.2
  491.2 4.1 collective-permute-done.1
  495.3 0.6 gather_fusion.1
  495.9 1.0 copy.12
  496.9 0.0 all-gather.4.cloned.1.call-update
  496.9 0.0 all-gather.8.cloned.1.call-start
  497.0 0.8 dynamic_slice.26
  497.7 0.8 dynamic_slice.25
  498.5 0.8 dynamic_slice.27
  499.3 16.5 %reduce-scatter.5.cloned.1.call-done = f32[128,256]{1,0:T(8,128)} async-done(((f32[1024,256]{1,0:T(8,128)}), f32[128,256]{1,0:T(8,128)}) %reduce-scatter.5.cloned.1.call-update) | async-done | bytes 131088 | tf_op jit(solution)/shard_map/reduce_scatter | solution.py:94
  515.8 1.0 fusion.3
  516.8 16.1 %all_gather.14 = f32[128,1024]{1,0:T(8,128)} all-gather(f32[128,256]{1,0:T(8,128)S(1)} %fusion.3), channel_id=1, replica_groups=mesh['harm'=8,'mode'=4] {'mode'}, dimensions={1}, use_global_device_ids=true | all-gather | bytes 655360 | tf_op jit(solution)/shard_map/all_gather | solution.py:102
  532.9 0.0 all-gather.8.cloned.1.call-update
  532.9 21.8 %all-gather.4.cloned.1.call-done = f32[1024,1024]{0,1:T(8,128)} async-done(((f32[128,1024]{0,1:T(8,128)}), f32[1024,1024]{0,1:T(8,128)}) %all-gather.4.cloned.1.call-update) | async-done | bytes 4194320 | tf_op jit(solution)/shard_map/spread_weights/all_gather | solution.py:73
  554.8 38.4 %all-gather.8.cloned.1.call-done = f32[1024,1024]{1,0:T(8,128)} async-done(((f32[128,1024]{1,0:T(8,128)}), f32[1024,1024]{1,0:T(8,128)}) %all-gather.8.cloned.1.call-update) | async-done | bytes 4194320 | tf_op jit(solution)/shard_map/all_gather | solution.py:103
  593.2 16.6 %fusion.7 = f32[1024,1024]{1,0:T(8,128)S(1)} fusion(f32[1024,1024]{0,1:T(8,128)} %all-gather.4.cloned.1.call-done, f32[1024,1024]{1,0:T(8,128)} %all-gather.8.cloned.1.call-done), kind=kOutput, calls=%fused_computation.24 | convolution fusion | flops 12884901888 | bytes 12582912 | tf_op jit(solution)/shard_map/dot_general | solution.py:33
  609.8 85.2 %fusion.8 = f32[1024,6144]{1,0:T(8,128)} fusion(f32[1024,1024]{1,0:T(8,128)S(1)} %fusion.7, f32[6144,1024]{1,0:T(8,128)} %all-gather.6.cloned.1.call-done), kind=kOutput, calls=%fused_computation.25 | convolution fusion | flops 77309411328 | bytes 54525952 | tf_op jit(solution)/shard_map/dot_general | solution.py:33
  (13 shorter events, 0.1 us)
Async XLA Ops:
  7.4 0.8 copy-start
  7.4 430.3 %all-gather.6.cloned.1.call-start = ((), (), s32[]{:S(2)}) async-start(), calls=%async_computation.4 | async-start | bytes 31457280 | tf_op jit(solution)/shard_map/all_gather | solution.py:91
  8.1 473.6 %reduce-scatter.3.cloned.1.call-start = ((), (), s32[]{:S(2)}) async-start(), calls=%async_computation.2 | async-start | bytes 4718592 | tf_op jit(solution)/shard_map/sum_weights/reduce_scatter | solution.py:68
  32.7 483.1 %reduce-scatter.5.cloned.1.call-start = ((), (), s32[]{:S(2)}) async-start(), calls=%async_computation.5 | async-start | bytes 1179648 | tf_op jit(solution)/shard_map/reduce_scatter | solution.py:94
  481.6 73.2 %all-gather.4.cloned.1.call-start = ((), (), s32[]{:S(2)}) async-start(), calls=%async_computation.3 | async-start | bytes 4718592 | tf_op jit(solution)/shard_map/spread_weights/all_gather | solution.py:73
  482.8 8.4 %collective-permute-start.2 = (f32[1,128,256]{2,1,0:T(8,128)S(1)}, f32[1,128,256]{2,1,0:T(8,128)S(1)}, u32[]{:S(2)}, u32[]{:S(2)}) collective-permute-start(f32[1,128,256]{2,1,0:T(8,128)S(1)} %get-tuple-element.6), channel_id=1, source_target_pairs={{0,3},{1,2},{2,1},{3,0},{4,7},{5,6},{6,5},{7,4},{8,11},{9,10},{10,... | collective-permute-start | bytes 393224 | tf_op jit(solution)/shard_map/swap/ppermute | solution.py:27
  483.2 12.1 %collective-permute-start.1 = (f32[1,128,256]{2,1,0:T(8,128)S(1)}, f32[1,128,256]{2,1,0:T(8,128)S(1)}, u32[]{:S(2)}, u32[]{:S(2)}) collective-permute-start(f32[1,128,256]{2,1,0:T(8,128)S(1)} %get-tuple-element.7), channel_id=1, source_target_pairs={{0,2},{1,3},{2,0},{3,1},{4,6},{5,7},{6,4},{7,5},{8,10},{9,11},{10,... | collective-permute-start | bytes 393224 | tf_op jit(solution)/shard_map/swap/ppermute | solution.py:27
  483.6 11.7 %collective-permute-start = (f32[1,128,256]{2,1,0:T(8,128)S(1)}, f32[1,128,256]{2,1,0:T(8,128)S(1)}, u32[]{:S(2)}, u32[]{:S(2)}) collective-permute-start(f32[1,128,256]{2,1,0:T(8,128)S(1)} %get-tuple-element.8), channel_id=1, source_target_pairs={{0,1},{1,0},{2,3},{3,2},{4,5},{5,4},{6,7},{7,6},{8,9},{9,8},{10,11... | collective-permute-start | bytes 393224 | tf_op jit(solution)/shard_map/swap/ppermute | solution.py:27
  496.9 96.2 %all-gather.8.cloned.1.call-start = ((), (), s32[]{:S(2)}) async-start(), calls=%async_computation.6 | async-start | bytes 4718592 | tf_op jit(solution)/shard_map/all_gather | solution.py:103
Sparse Core Ops, SparseCore 0:
  9.7 427.8 all-gather.5
Sparse Core Ops, SparseCore 1:
  32.8 53.7 reduce-scatter.2
  481.6 34.1 reduce-scatter.4
  517.5 37.2 all-gather.3
  556.7 36.4 all-gather.7
